TPU v7x, 32 devices: a whole 2x2x4 slice. The times are simulated.
32 devices in a mesh: dp: 8 (over z, x), tensor: 4 (over y, core).
Axes of the slice: x: 2, y: 2, z: 4, core: 2. Of those that a mesh axis runs over, the one named last changes fastest.
Arguments:
- tokens: bfloat16 [20480, 768], P(('dp', 'tensor')), may hold values from -6 to 6
- segment_ids: int32 [20480], P('dp'), may hold values from 0 to 8, as said below
- lengths: int32 [40], P('dp'), may hold values from 410 to 512, as said below
- w_query: bfloat16 [768, 768], P(None, 'tensor'), may hold values from -0.21875 to 0.21875
- b_query: float32 [768], P('tensor'), may hold values from -3 to 3
- w_key: bfloat16 [768, 768], P(None, 'tensor'), may hold values from -0.21875 to 0.21875
- w_value: bfloat16 [768, 768], P(None, 'tensor'), may hold values from -0.21875 to 0.21875
- b_value: float32 [768], P('tensor'), may hold values from -3 to 3
- w_output: bfloat16 [768, 768], P('tensor'), may hold values from -1.5 to 1.5
- b_output: float32 [768], replicated, may hold values from -2 to 2
- first_gain: float32 [768], replicated, may hold values from 0.5 to 1.5
- first_shift: float32 [768], replicated, may hold values from -2 to 2
- w_inner: bfloat16 [768, 3072], P(None, 'tensor'), may hold values from -0.21875 to 0.21875
- b_inner: float32 [3072], P('tensor'), may hold values from -3 to 3
- w_outer: bfloat16 [3072, 768], P('tensor'), may hold values from -0.109375 to 0.109375
- b_outer: float32 [768], replicated, may hold values from -2 to 2
- second_gain: float32 [768], replicated, may hold values from 0.5 to 1.5
- second_shift: float32 [768], replicated, may hold values from -2 to 2
- cotangent: bfloat16 [20480, 768], P(('dp', 'tensor')), may hold values from -6 to 6
Outputs:
- output: bfloat16 [20480, 768], P(('dp', 'tensor'))
- grad_tokens: bfloat16 [20480, 768], P(('dp', 'tensor'))
- grad_w_query: float32 [768, 768], P(None, 'tensor')
- grad_b_query: float32 [768], P('tensor')
- grad_w_key: float32 [768, 768], P(None, 'tensor')
- grad_w_value: float32 [768, 768], P(None, 'tensor')
- grad_b_value: float32 [768], P('tensor')
- grad_w_output: float32 [768, 768], P('tensor')
- grad_b_output: float32 [768], P('tensor')
- grad_first_gain: float32 [768], P('tensor')
- grad_first_shift: float32 [768], P('tensor')
- grad_w_inner: float32 [768, 3072], P(None, 'tensor')
- grad_b_inner: float32 [3072], P('tensor')
- grad_w_outer: float32 [3072, 768], P('tensor')
- grad_b_outer: float32 [768], P('tensor')
- grad_second_gain: float32 [768], P('tensor')
- grad_second_shift: float32 [768], P('tensor')
Inputs may be any that keep to these rules, and one draw needn't show every extreme that they name: `segment_ids`: along each packed sequence of 512 positions the ids start at 0, never fall, and rise by at most one a position; the first sequence reaches the largest id. `lengths`: live positions of each packed sequence; the first sequence is full.
All inputs are finite; a program needn't handle non-finite values.
Results may differ from a plain program's by a relative error of at most 0.019.
Values may be sent and summed in bfloat16 or wider, within the bound.
A program may use at most 128 MiB of HBM per device.

v0:
```python
import math
import jax
import jax.numpy as jnp
from jax import lax
from jax.sharding import PartitionSpec as P

HD = 64
LEN = 512
EPSILON = 1e-12
NEGATIVE = -1000000000.0


def normalize(value, gain, shift):
    average = jnp.mean(value, axis=-1, keepdims=True)
    centered = value - average
    variance = jnp.mean(centered * centered, axis=-1, keepdims=True)
    inverse = lax.rsqrt(variance + EPSILON)
    unit = centered * inverse
    return (unit * gain + shift, unit, inverse)


def norm_backward(grad, unit, inverse, gain):
    scaled = grad * gain
    first_mean = jnp.mean(scaled, axis=-1, keepdims=True)
    second_mean = jnp.mean(scaled * unit, axis=-1, keepdims=True)
    result = inverse * (scaled - first_mean - unit * second_mean)
    return (result, jnp.sum(grad * unit, axis=0), jnp.sum(grad, axis=0))


def gelu_value(inner):
    return 0.5 * inner * (1.0 + lax.erf(inner * (1.0 / math.sqrt(2.0))))


def gelu_slope(inner):
    cumulative = 0.5 * (1.0 + lax.erf(inner * (1.0 / math.sqrt(2.0))))
    return cumulative + inner * jnp.exp(-0.5 * inner * inner) * (1.0 / math.sqrt(2.0 * math.pi))


def allowed_mask(segments, length):
    places = jnp.arange(segments.shape[0])
    same = segments[:, None] == segments[None, :]
    live = places[None, :] < length
    return same & live | (places[:, None] == places[None, :])


def split_heads(rows):
    return rows.reshape(rows.shape[0], rows.shape[1] // HD, HD)


def attention_logits(query_rows, key_rows, segments, length):
    scores = jnp.einsum(
        "qhd,khd->hqk",
        split_heads(query_rows),
        split_heads(key_rows),
        preferred_element_type=jnp.float32,
    )
    return jnp.where(allowed_mask(segments, length)[None], scores * (1.0 / math.sqrt(HD)), NEGATIVE)


def forward_attend(block):
    query_rows, key_rows, value_rows, segments, length = block
    logits = attention_logits(query_rows, key_rows, segments, length)
    peak = jnp.max(logits, axis=-1, keepdims=True)
    powers = jnp.exp(logits - peak)
    total = jnp.sum(powers, axis=-1, keepdims=True)
    weights = (powers / total).astype(jnp.bfloat16)
    context = jnp.einsum(
        "hqk,khd->qhd", weights, split_heads(value_rows), preferred_element_type=jnp.float32
    )
    log_total = (peak + jnp.log(total))[..., 0]
    return (context.reshape(query_rows.shape).astype(jnp.bfloat16), log_total)


def backward_attend(block):
    query_rows, key_rows, value_rows, grad_rows, segments, length, log_total = block
    logits = attention_logits(query_rows, key_rows, segments, length)
    probs = jnp.exp(logits - log_total[..., None])
    grad_heads = split_heads(grad_rows)
    grad_probs = jnp.einsum(
        "qhd,khd->hqk", grad_heads, split_heads(value_rows), preferred_element_type=jnp.float32
    )
    across = jnp.sum(probs * grad_probs, axis=-1, keepdims=True)
    grad_scores = (probs * (grad_probs - across) * (1.0 / math.sqrt(HD))).astype(jnp.bfloat16)
    grad_query = jnp.einsum(
        "hqk,khd->qhd", grad_scores, split_heads(key_rows), preferred_element_type=jnp.float32
    )
    grad_key = jnp.einsum(
        "hqk,qhd->khd", grad_scores, split_heads(query_rows), preferred_element_type=jnp.float32
    )
    grad_value = jnp.einsum(
        "hqk,qhd->khd", probs.astype(jnp.bfloat16), grad_heads, preferred_element_type=jnp.float32
    )
    shape = query_rows.shape
    joined = jnp.concatenate(
        [grad_query.reshape(shape), grad_key.reshape(shape), grad_value.reshape(shape)], axis=1
    )
    return joined.astype(jnp.bfloat16)


def shards(
    tokens,
    segment_ids,
    lengths,
    w_query,
    b_query,
    w_key,
    w_value,
    b_value,
    w_output,
    b_output,
    first_gain,
    first_shift,
    w_inner,
    b_inner,
    w_outer,
    b_outer,
    second_gain,
    second_shift,
    cotangent,
):
    parts = lax.axis_size("tensor")
    width = w_query.shape[1]
    count = segment_ids.shape[0] // LEN
    joined = jnp.concatenate([w_query, w_key, w_value], axis=1)

    def by_sequence(rows_all):
        return rows_all.reshape(count, LEN, rows_all.shape[1])

    whole = lax.all_gather(tokens, "tensor", axis=0, tiled=True)
    projected = jnp.dot(whole, joined, preferred_element_type=jnp.float32)
    query_rows = (projected[:, :width] + b_query).astype(jnp.bfloat16)
    key_rows = projected[:, width : 2 * width].astype(jnp.bfloat16)
    value_rows = (projected[:, 2 * width :] + b_value).astype(jnp.bfloat16)
    segments = segment_ids.reshape(count, LEN)
    context, log_total = lax.map(
        forward_attend,
        (
            by_sequence(query_rows),
            by_sequence(key_rows),
            by_sequence(value_rows),
            segments,
            lengths,
        ),
    )
    context = context.reshape(count * LEN, width)
    piece = context
    attended = lax.psum_scatter(
        jnp.dot(piece, w_output, preferred_element_type=jnp.float32),
        "tensor",
        scatter_dimension=0,
        tiled=True,
    )
    first_full, first_unit, first_inverse = normalize(
        tokens.astype(jnp.float32) + attended + b_output, first_gain, first_shift
    )
    first_out = first_full.astype(jnp.bfloat16)
    ffn_rows = lax.all_gather(first_out, "tensor", axis=0, tiled=True)
    inner = jnp.dot(ffn_rows, w_inner, preferred_element_type=jnp.float32) + b_inner
    hidden = gelu_value(inner).astype(jnp.bfloat16)
    piece = hidden
    feed_out = lax.psum_scatter(
        jnp.dot(piece, w_outer, preferred_element_type=jnp.float32).astype(jnp.bfloat16),
        "tensor",
        scatter_dimension=0,
        tiled=True,
    ).astype(jnp.float32)
    second_full, second_unit, second_inverse = normalize(
        first_out.astype(jnp.float32) + feed_out + b_outer, second_gain, second_shift
    )
    output = second_full.astype(jnp.bfloat16)
    grad_second, grad_second_gain, grad_second_shift = norm_backward(
        cotangent.astype(jnp.float32), second_unit, second_inverse, second_gain
    )
    grad_feed = grad_second.astype(jnp.bfloat16)
    grad_b_outer = jnp.sum(grad_feed.astype(jnp.float32), axis=0)
    feed_grads = lax.all_gather(grad_feed, "tensor", axis=0, tiled=True)
    grad_w_outer = jnp.einsum("gf,gd->fd", hidden, feed_grads, preferred_element_type=jnp.float32)
    grad_hidden = jnp.einsum("gd,fd->gf", feed_grads, w_outer, preferred_element_type=jnp.float32)
    grad_inner = (grad_hidden * gelu_slope(inner)).astype(jnp.bfloat16)
    grad_b_inner = jnp.sum(grad_inner.astype(jnp.float32), axis=0)
    grad_w_inner = jnp.einsum("gd,gf->df", ffn_rows, grad_inner, preferred_element_type=jnp.float32)
    piece = grad_inner
    grad_first = grad_second + lax.psum_scatter(
        jnp.einsum("gf,df->gd", piece, w_inner, preferred_element_type=jnp.float32).astype(
            jnp.bfloat16
        ),
        "tensor",
        scatter_dimension=0,
        tiled=True,
    ).astype(jnp.float32)
    grad_branch_full, grad_first_gain, grad_first_shift = norm_backward(
        grad_first, first_unit, first_inverse, first_gain
    )
    grad_branch = grad_branch_full.astype(jnp.bfloat16)
    grad_b_output = jnp.sum(grad_branch.astype(jnp.float32), axis=0)
    branch_rows = lax.all_gather(grad_branch, "tensor", axis=0, tiled=True)
    grad_w_output = jnp.einsum(
        "gc,gd->cd", context, branch_rows, preferred_element_type=jnp.float32
    )
    grad_context = jnp.einsum(
        "gd,cd->gc", branch_rows, w_output, preferred_element_type=jnp.float32
    ).astype(jnp.bfloat16)
    grad_joined = lax.map(
        backward_attend,
        (
            by_sequence(query_rows),
            by_sequence(key_rows),
            by_sequence(value_rows),
            by_sequence(grad_context),
            segments,
            lengths,
            log_total,
        ),
    )
    grad_joined = grad_joined.reshape(count * LEN, 3 * width)
    grad_w_joined = jnp.einsum("gd,gc->dc", whole, grad_joined, preferred_element_type=jnp.float32)
    grad_bias_all = jnp.sum(grad_joined.astype(jnp.float32), axis=0)
    grad_b_query = grad_bias_all[:width]
    grad_b_value = grad_bias_all[2 * width :]
    input_terms = jnp.einsum("gc,dc->gd", grad_joined, joined, preferred_element_type=jnp.float32)
    small = jnp.stack(
        [
            grad_b_output,
            grad_first_gain,
            grad_first_shift,
            grad_b_outer,
            grad_second_gain,
            grad_second_shift,
        ]
    )
    small_flat = small.reshape(6, parts, small.shape[1] // parts).transpose(1, 0, 2).reshape(-1)
    input_share, small_share = (
        lax.psum_scatter(
            input_terms.astype(jnp.bfloat16), "tensor", scatter_dimension=0, tiled=True
        ).astype(jnp.float32),
        lax.psum_scatter(
            small_flat.astype(jnp.bfloat16), "tensor", scatter_dimension=0, tiled=True
        ).astype(jnp.float32),
    )
    grad_tokens = (grad_branch_full + input_share).astype(jnp.bfloat16)
    small_share = small_share.reshape(6, small_share.shape[0] // 6)
    (
        grad_w_joined,
        grad_b_query,
        grad_b_value,
        grad_w_output,
        grad_w_inner,
        grad_b_inner,
        grad_w_outer,
        small_share,
    ) = lax.psum(
        (
            grad_w_joined,
            grad_b_query,
            grad_b_value,
            grad_w_output,
            grad_w_inner,
            grad_b_inner,
            grad_w_outer,
            small_share,
        ),
        "dp",
    )
    return (
        output,
        grad_tokens,
        grad_w_joined[:, :width],
        grad_b_query,
        grad_w_joined[:, width : 2 * width],
        grad_w_joined[:, 2 * width :],
        grad_b_value,
        grad_w_output,
        small_share[0],
        small_share[1],
        small_share[2],
        grad_w_inner,
        grad_b_inner,
        grad_w_outer,
        small_share[3],
        small_share[4],
        small_share[5],
    )


def solution(mesh):
    in_specs = (
        P(("dp", "tensor"), None),
        P("dp"),
        P("dp"),
        P(None, "tensor"),
        P("tensor"),
        P(None, "tensor"),
        P(None, "tensor"),
        P("tensor"),
        P("tensor", None),
        P(),
        P(),
        P(),
        P(None, "tensor"),
        P("tensor"),
        P("tensor", None),
        P(),
        P(),
        P(),
        P(("dp", "tensor"), None),
    )
    out_specs = (
        P(("dp", "tensor"), None),
        P(("dp", "tensor"), None),
        P(None, "tensor"),
        P("tensor"),
        P(None, "tensor"),
        P(None, "tensor"),
        P("tensor"),
        P("tensor", None),
        P("tensor"),
        P("tensor"),
        P("tensor"),
        P(None, "tensor"),
        P("tensor"),
        P("tensor", None),
        P("tensor"),
        P("tensor"),
        P("tensor"),
    )
    return jax.shard_map(shards, mesh=mesh, in_specs=in_specs, out_specs=out_specs, check_vma=False)
```

profile of v0, /device:TPU:0, one launch (start us, length us, event | category | flops | bytes accessed | tf_op | source)
XLA Modules:
  0.0 826.7 jit_solution(1804968826815909880)
XLA Ops:
  10.7 34.6 %all-gather.5.cloned.1.call-done = bf16[2560,768]{1,0:T(8,128)(2,1)} async-done(((bf16[640,768]{1,0:T(8,128)(2,1)}), bf16[2560,768]{1,0:T(8,128)(2,1)}) %all-gather.5.cloned.1.call-update) | async-done | bytes 3932176 | tf_op jit(solution)/shard_map/all_gather | solution.py:129
  45.3 4.6 convolution_bitcast_fusion
  60.1 37.0 %while.22 = (s32[]{:T(128)}, bf16[5,512,192]{1,2,0:T(8,128)(2,1)S(1)}, f32[5,3,512]{2,1,0:T(4,128)}, bf16[5,512,192]{1,2,0:T(8,128)(2,1)}, s32[5,512]{1,0:T(8,12...) while((s32[]{:T(128)}, ...), condition=%wide.region_3.4_spmd, body=%wide.region_0.3_spmd.sunk | while | flops 211909632 | bytes 12903561 | solution.py:135
  97.7 5.4 fusion.60
  103.2 69.1 %reduce-scatter.5.cloned.1.call-done = f32[640,768]{1,0:T(8,128)} async-done(((f32[2560,768]{1,0:T(8,128)}), f32[640,768]{1,0:T(8,128)}) %reduce-scatter.5.cloned.1.call-update) | async-done | bytes 1966096 | tf_op jit(solution)/shard_map/reduce_scatter | solution.py:147
  177.0 32.6 %all-gather.7.cloned.1.call-done = bf16[2560,768]{1,0:T(8,128)(2,1)} async-done(((bf16[640,768]{1,0:T(8,128)(2,1)}), bf16[2560,768]{1,0:T(8,128)(2,1)}) %all-gather.7.cloned.1.call-update) | async-done | bytes 3932176 | tf_op jit(solution)/shard_map/all_gather | solution.py:157
  209.6 7.5 multiply_convert_fusion.1
  219.0 4.7 convolution_convert_fusion.1
  223.8 43.0 %reduce-scatter.7.cloned.1.call-done = bf16[640,768]{1,0:T(8,128)(2,1)} async-done(((bf16[2560,768]{1,0:T(8,128)(2,1)}), bf16[640,768]{1,0:T(8,128)(2,1)}) %reduce-scatter.7.cloned.1.call-update) | async-done | bytes 983056 | tf_op jit(solution)/shard_map/reduce_scatter | solution.py:161
  276.5 33.1 %all-gather.9.cloned.1.call-done = bf16[2560,768]{1,0:T(8,128)(2,1)} async-done(((bf16[640,768]{1,0:T(8,128)(2,1)}), bf16[2560,768]{1,0:T(8,128)(2,1)}) %all-gather.9.cloned.1.call-update) | async-done | bytes 3932176 | tf_op jit(solution)/shard_map/all_gather | solution.py:176
  309.6 9.6 %convert_reduce_fusion = (f32[768]{0:T(1024)}, bf16[2560,768]{1,0:T(8,128)(2,1)S(1)}) fusion(f32[2560,768]{1,0:T(8,128)} %get-tuple-element.259, f32[768]{0:T(1024)S(1)} %copy-done.37, bf16[2560,768]{1,0:T(8,128)(2,1)} %all-gather.9.cloned.1.call-done, bf16[768,768]{1,0:T(8,128)(2,1)} %param.37), kind=kOutput, calls=%fused_computation.53 | convolution fusion | flops 3045457152 | bytes 16914432 | tf_op jit(solution)/shard_map/gd,fd->gf/dot_general | solution.py:178
  321.1 4.8 convolution_convert_fusion
  326.1 42.8 %reduce-scatter.9.cloned.1.call-done = bf16[640,768]{1,0:T(8,128)(2,1)} async-done(((bf16[2560,768]{1,0:T(8,128)(2,1)}), bf16[640,768]{1,0:T(8,128)(2,1)}) %reduce-scatter.9.cloned.1.call-update) | async-done | bytes 983056 | tf_op jit(solution)/shard_map/reduce_scatter | solution.py:183
  375.4 8.1 fusion.63
  383.6 4.8 fusion.62
  388.4 20.1 %all-gather.11.cloned.1.call-done = bf16[2560,768]{1,0:T(8,128)(2,1)} async-done(((bf16[640,768]{1,0:T(8,128)(2,1)}), bf16[2560,768]{1,0:T(8,128)(2,1)}) %all-gather.11.cloned.1.call-update) | async-done | bytes 3932176 | tf_op jit(solution)/shard_map/all_gather | solution.py:196
  414.2 102.7 %while.23 = (s32[]{:T(128)}, bf16[5,512,576]{1,2,0:T(8,128)(2,1)}, bf16[5,512,192]{1,2,0:T(8,128)(2,1)}, s32[5,512]{1,0:T(8,128)S(1)}, s32[5]{0:T(128)}, /*index...) while((s32[]{:T(128)}, bf16[5,512,576]{1,2,0:T(8,128)(2,1)}, ...), condition=%wide.region_17.18_spmd, body=%wide.region_15.17_spmd.sunk | while | flops 517444096 | bytes 28075180 | solution.py:203
  423.8 4.7 fusion.141
  428.4 4.4 fusion.140
  444.3 4.7 fusion.141
  464.8 4.7 fusion.141
  469.5 4.4 fusion.140
  485.4 4.7 fusion.141
  506.0 4.7 fusion.141
  510.6 4.4 fusion.140
  516.9 4.8 copy.98
  525.8 6.0 convolution_bitcast_fusion.1
  533.7 5.8 convolution_convert_fusion.2
  542.1 11.0 %all-reduce = bf16[4608]{0:T(1024)(128)(2,1)S(1)} all-reduce(bf16[4608]{0:T(1024)(128)(2,1)S(1)} %convert_element_type.135), channel_id=6, replica_groups=mesh['dp'=8,'tensor'=4] {'tensor'}, use_global_device_ids=true, to_apply=%region_30.31.clone | all-reduce | flops 4608 | bytes 18432
  553.7 40.0 %all-reduce.1 = (f32[192]{0:T(256)}, f32[192]{0:T(256)}, f32[6,192]{1,0:T(8,128)S(1)}, f32[768]{0:T(1024)}) all-reduce(f32[192]{0:T(256)S(1)} %get-tuple-element.257, f32[192]{0:T(256)S(1)} %get-tuple-element.256, f32[6,192]{1,0:T(8,128)S(1)} %reshape.391, f32[768]{0:T(1024)S(1)} %copy-done.31), channel_id=1, replica_groups=mesh['dp'=8,'tensor'=4] {'dp'}, use_global_device_ids=true, to_apply=%region_21.22 | all-reduce | flops 2304 | bytes 18432 | tf_op jit(solution)/shard_map/psum | solution.py:251
  594.3 174.0 %all-reduce.5.cloned.1.call-done = (f32[768,576]{0,1:T(8,128)}, f32[192,768]{1,0:T(8,128)}, f32[768,768]{1,0:T(8,128)}, f32[768,768]{1,0:T(8,128)}) async-done(((f32[768,576]{0,1:T(8,128)}, f32[192,768]{1,0:T(8,128)}, f32[768,768]{1,0:T(8,128)}, f32[768,768]{1,0:T(8,128)}), (f32[768,576]{0,1:T(8,128)}, f32[192,768]{1,0:T(8,128)}, f32[768,768]{1,0:T(8,128)}, ...) | async-done | bytes 7077904 | tf_op jit(solution)/shard_map/psum | solution.py:251
  770.9 41.8 %reduce-scatter.11.cloned.1.call-done = bf16[640,768]{1,0:T(8,128)(2,1)} async-done(((bf16[2560,768]{1,0:T(8,128)(2,1)}), bf16[640,768]{1,0:T(8,128)(2,1)}) %reduce-scatter.11.cloned.1.call-update) | async-done | bytes 983056 | tf_op jit(solution)/shard_map/reduce_scatter | solution.py:233
  (283 shorter events, 166.3 us)
Async XLA Ops:
  7.2 202.4 %copy-start = (bf16[768,768]{1,0:T(8,128)(2,1)S(1)}, bf16[768,768]{1,0:T(8,128)(2,1)}, u32[]{:S(2)}) copy-start(bf16[768,768]{1,0:T(8,128)(2,1)} %param.35) | copy-start | bytes 3538948
  7.2 3.5 copy-start.18
  7.2 38.1 %all-gather.5.cloned.1.call-start = ((), (), s32[]{:S(2)}) async-start(), calls=%async_computation.4 | async-start | bytes 4915200 | tf_op jit(solution)/shard_map/all_gather | solution.py:129
  7.9 164.3 %reduce-scatter.5.cloned.1.call-start = ((), (), s32[]{:S(2)}) async-start(), calls=%async_computation.5 | async-start | bytes 9830400 | tf_op jit(solution)/shard_map/reduce_scatter | solution.py:147
  10.7 39.2 %copy-start.21 = (bf16[768,576]{0,1:T(8,128)(2,1)}, bf16[768,576]{0,1:T(8,128)(2,1)S(1)}, u32[]{:S(2)}) copy-start(bf16[768,576]{0,1:T(8,128)(2,1)S(1)} %constant_dynamic-update-slice_fusion.1) | copy-start | bytes 2654212
  97.7 5.4 copy-start.6
  103.1 69.2 %copy-start.30 = (f32[768]{0:T(1024)S(1)}, f32[768]{0:T(1024)}, u32[]{:S(2)}) copy-start(f32[768]{0:T(1024)} %param.32) | copy-start | bytes 9220
  103.1 106.5 %all-gather.7.cloned.1.call-start = ((), (), s32[]{:S(2)}) async-start(), calls=%async_computation.6 | async-start | bytes 4915200 | tf_op jit(solution)/shard_map/all_gather | solution.py:157
  175.1 34.5 %copy-start.37 = (f32[768]{0:T(1024)S(1)}, f32[768]{0:T(1024)}, u32[]{:S(2)}) copy-start(f32[768]{0:T(1024)} %param.36) | copy-start | bytes 9220
  176.5 90.3 %reduce-scatter.7.cloned.1.call-start = ((), (), s32[]{:S(2)}) async-start(), calls=%async_computation.7 | async-start | bytes 4915200 | tf_op jit(solution)/shard_map/reduce_scatter | solution.py:161
  209.6 9.4 %copy-start.36 = (bf16[768,768]{1,0:T(8,128)(2,1)S(1)}, bf16[768,768]{1,0:T(8,128)(2,1)}, u32[]{:S(2)}) copy-start(bf16[768,768]{1,0:T(8,128)(2,1)} %param.37) | copy-start | bytes 3538948
  223.7 43.1 %copy-start.22 = (f32[768]{0:T(1024)S(1)}, f32[768]{0:T(1024)}, u32[]{:S(2)}) copy-start(f32[768]{0:T(1024)} %param.38) | copy-start | bytes 9220
  223.8 85.9 %all-gather.9.cloned.1.call-start = ((), (), s32[]{:S(2)}) async-start(), calls=%async_computation.8 | async-start | bytes 4915200 | tf_op jit(solution)/shard_map/all_gather | solution.py:176
  276.5 92.5 %reduce-scatter.9.cloned.1.call-start = ((), (), s32[]{:S(2)}) async-start(), calls=%async_computation.9 | async-start | bytes 4915200 | tf_op jit(solution)/shard_map/reduce_scatter | solution.py:183
  325.9 82.6 %all-gather.11.cloned.1.call-start = ((), (), s32[]{:S(2)}) async-start(), calls=%async_computation.10 | async-start | bytes 4915200 | tf_op jit(solution)/shard_map/all_gather | solution.py:196
  369.0 3.5 copy-start.2
  369.0 3.5 copy-start.9
  375.4 392.9 %all-reduce.5.cloned.1.call-start = ((), (), s32[]{:S(2)}) async-start(), calls=%async_computation.12 | async-start | bytes 14155776 | tf_op jit(solution)/shard_map/psum | solution.py:251
  375.4 8.2 copy-start.35
  375.4 8.2 copy-start.41
  383.6 24.9 %copy-start.17 = (bf16[192,768]{1,0:T(8,128)(2,1)S(1)}, bf16[192,768]{1,0:T(8,128)(2,1)}, u32[]{:S(2)}) copy-start(bf16[192,768]{1,0:T(8,128)(2,1)} %param.31) | copy-start | bytes 884740
  516.9 4.8 copy-start.7
  521.7 4.0 copy-start.11
  531.8 280.9 %reduce-scatter.11.cloned.1.call-start = ((), (), s32[]{:S(2)}) async-start(), calls=%async_computation.11 | async-start | bytes 4915200 | tf_op jit(solution)/shard_map/reduce_scatter | solution.py:233
  539.5 2.3 copy-start.29
  539.6 13.7 %copy-start.4 = (bf16[5,512,576]{1,2,0:T(8,128)(2,1)S(1)}, bf16[5,512,576]{1,2,0:T(8,128)(2,1)}, u32[]{:S(2)}) copy-start(bf16[5,512,576]{1,2,0:T(8,128)(2,1)} %get-tuple-element.109) | copy-start | bytes 8847364
  539.6 14.1 %copy-start.31 = (f32[768]{0:T(1024)S(1)}, f32[768]{0:T(1024)}, u32[]{:S(2)}) copy-start(f32[768]{0:T(1024)} %get-tuple-element.260) | copy-start | bytes 9220
  553.7 259.0 %copy-start.5 = (f32[640,768]{1,0:T(8,128)S(1)}, f32[640,768]{1,0:T(8,128)}, u32[]{:S(2)}) copy-start(f32[640,768]{1,0:T(8,128)} %get-tuple-element.232) | copy-start | bytes 5898244
  812.7 2.5 copy-start.16
  812.7 3.3 copy-start.14
  816.1 2.5 copy-start.13
  816.1 3.9 copy-start.1
  (23 other events, 30.7 us)
Sparse Core Ops, SparseCore 0:
  9.6 35.6 all-gather.4
  103.2 68.9 reduce-scatter.4
  176.6 32.9 all-gather.6
  223.9 42.8 reduce-scatter.6
  276.6 32.9 all-gather.8
  326.0 42.8 reduce-scatter.8
  375.5 32.9 all-gather.10
  531.9 236.3 all-reduce.4
  770.8 41.8 reduce-scatter.10
where the time goes:
time: 835 us; the launch traced here: 827 us
  waiting for transfers between devices  492 us (59%)
  matrix products  143 us (17%)
  local copies, waits for them, and re-layouts  75.5 us (9%)
  blocking collectives  50.9 us (6%)
  other arithmetic  48.9 us (6%)
  between operations  15.1 us (2%)
    psum x1, waiting for transfers between devices, shards(): lax.psum((grad_w_joined, grad_b_query, grad_b_value, grad_w_output, grad_...  174 us
    reduce_scatter x1, waiting for transfers between devices, shards(): lax.psum_scatter(jnp.dot(piece, w_output, preferred_element_type=jnp.floa...  69.1 us
    reduce_scatter x1, waiting for transfers between devices, shards(): lax.psum_scatter(jnp.dot(piece, w_outer, preferred_element_type=jnp.float...  43 us
    reduce_scatter x1, waiting for transfers between devices, shards(): lax.psum_scatter(jnp.einsum('gf,df->gd', piece, w_inner, preferred_elemen...  42.8 us
    reduce_scatter x1, waiting for transfers between devices, shards(): lax.psum_scatter(input_terms.astype(jnp.bfloat16), 'tensor', scatter_dime...  41.8 us
    psum x1, blocking collectives, shards(): lax.psum((grad_w_joined, grad_b_query, grad_b_value, grad_w_output, grad_...  40 us
    all_gather x1, waiting for transfers between devices, shards(): whole = lax.all_gather(tokens, 'tensor', axis=0, tiled=True)  34.6 us
    all_gather x1, waiting for transfers between devices, shards(): feed_grads = lax.all_gather(grad_feed, 'tensor', axis=0, tiled=True)  33.1 us
  transfers between devices with their start and end apart: 9, of which 9 were waited for; matrix products, arithmetic and copies ran while one was open for 3% of the time, Pallas kernels for 0%

commit v1 on v0

--- a/solution.py
+++ b/solution.py
@@ -8,6 +8,26 @@
 LEN = 512
 EPSILON = 1e-12
 NEGATIVE = -1000000000.0
+
+
+def ports_state(x0):
+    along_axis = "tensor"
+    k_now, later, block_now = (lax.axis_size(along_axis), lax.axis_index(along_axis), x0.shape[0])
+    local_now, current_arr = (x0, 1)
+    while current_arr < k_now:
+        local_now = jnp.concatenate(
+            [
+                local_now,
+                lax.ppermute(
+                    local_now,
+                    along_axis,
+                    tuple(((i, (i - current_arr) % k_now) for i in range(k_now))),
+                ),
+            ],
+            axis=0,
+        )
+        current_arr = 2 * current_arr
+    return jnp.roll(local_now, later * block_now, axis=0)
 
 
 def normalize(value, gain, shift):
@@ -154,7 +174,7 @@
         tokens.astype(jnp.float32) + attended + b_output, first_gain, first_shift
     )
     first_out = first_full.astype(jnp.bfloat16)
-    ffn_rows = lax.all_gather(first_out, "tensor", axis=0, tiled=True)
+    ffn_rows = ports_state(first_out)
     inner = jnp.dot(ffn_rows, w_inner, preferred_element_type=jnp.float32) + b_inner
     hidden = gelu_value(inner).astype(jnp.bfloat16)
     piece = hidden

time: 835 us -> 879 us (1.053)
  waiting for transfers between devices: 492 us -> 513 us
  local copies, waits for them, and re-layouts: 75.5 us -> 91.5 us
    ppermute x0 -> x2, waiting for transfers between devices: none -> 53.6 us  [ports_state(): lax.ppermute(local_now, along_axis, tuple(((i, (i - current_arr) % k_now)...]
    all_gather x1 -> x0, waiting for transfers between devices: 32.6 us -> none  [shards(): ffn_rows = lax.all_gather(first_out, 'tensor', axis=0, tiled=True)]
    unnamed x93 -> x97, local copies, waits for them, and re-layouts: 14.3 us -> 22.1 us
  transfers between devices with their start and end apart: 9 -> 10, of which waited for: 9 -> 10; matrix products, arithmetic and copies ran while one was open for 3% -> 3% of each run, Pallas kernels for 0% -> 0%
where the time goes in v1:
time: 879 us; the launch traced here: 870 us
  waiting for transfers between devices  513 us (58%)
  matrix products  142 us (16%)
  local copies, waits for them, and re-layouts  91.5 us (10%)
  other arithmetic  54.3 us (6%)
  blocking collectives  51 us (6%)
  between operations  15.4 us (2%)
    psum x1, waiting for transfers between devices, shards(): lax.psum((grad_w_joined, grad_b_query, grad_b_value, grad_w_output, grad_...  174 us
    reduce_scatter x1, waiting for transfers between devices, shards(): lax.psum_scatter(jnp.dot(piece, w_output, preferred_element_type=jnp.floa...  69.1 us
    ppermute x2, waiting for transfers between devices, ports_state(): lax.ppermute(local_now, along_axis, tuple(((i, (i - current_arr) % k_now)...  53.6 us
    reduce_scatter x1, waiting for transfers between devices, shards(): lax.psum_scatter(jnp.dot(piece, w_outer, preferred_element_type=jnp.float...  44.2 us
    reduce_scatter x1, waiting for transfers between devices, shards(): lax.psum_scatter(jnp.einsum('gf,df->gd', piece, w_inner, preferred_elemen...  42.8 us
    reduce_scatter x1, waiting for transfers between devices, shards(): lax.psum_scatter(input_terms.astype(jnp.bfloat16), 'tensor', scatter_dime...  41.7 us
    psum x1, blocking collectives, shards(): lax.psum((grad_w_joined, grad_b_query, grad_b_value, grad_w_output, grad_...  40 us
    all_gather x1, waiting for transfers between devices, shards(): whole = lax.all_gather(tokens, 'tensor', axis=0, tiled=True)  33.6 us
  transfers between devices with their start and end apart: 10, of which 10 were waited for; matrix products, arithmetic and copies ran while one was open for 3% of the time, Pallas kernels for 0%

profile of v1, /device:TPU:0, one launch (start us, length us, event | category | flops | bytes accessed | tf_op | source)
XLA Modules:
  0.0 870.3 jit_solution(7133655208353532817)
XLA Ops:
  11.7 33.6 %all-gather.4.cloned.1.call-done = bf16[2560,768]{1,0:T(8,128)(2,1)} async-done(((bf16[640,768]{1,0:T(8,128)(2,1)}), bf16[2560,768]{1,0:T(8,128)(2,1)}) %all-gather.4.cloned.1.call-update) | async-done | bytes 3932176 | tf_op jit(solution)/shard_map/all_gather | solution.py:149
  45.3 4.6 convolution_bitcast_fusion
  60.1 40.3 %while.22 = (s32[]{:T(128)}, bf16[5,512,192]{1,2,0:T(8,128)(2,1)}, f32[5,3,512]{2,1,0:T(4,128)}, bf16[5,512,192]{1,2,0:T(8,128)(2,1)}, s32[5,512]{1,0:T(8,128)S(...) while((s32[]{:T(128)}, bf16[5,512,192]{1,2,0:T(8,128)(2,1)}, ...), condition=%wide.region_3.4_spmd, body=%wide.region_0.3_spmd.sunk | while | flops 211909632 | bytes 12903561 | solution.py:155
  106.2 69.1 %reduce-scatter.5.cloned.1.call-done = f32[640,768]{1,0:T(8,128)} async-done(((f32[2560,768]{1,0:T(8,128)}), f32[640,768]{1,0:T(8,128)}) %reduce-scatter.5.cloned.1.call-update) | async-done | bytes 1966096 | tf_op jit(solution)/shard_map/reduce_scatter | solution.py:167
  180.1 11.9 %collective-permute-done = bf16[640,768]{1,0:T(8,128)(2,1)S(1)} collective-permute-done((bf16[640,768]{1,0:T(8,128)(2,1)}, bf16[640,768]{1,0:T(8,128)(2,1)S(1)}, u32[]{:S(2)}, u32[]{:S(2)}) %collective-permute-start) | collective-permute-done | bytes 983072 | tf_op jit(solution)/shard_map/ppermute | solution.py:21
  199.2 41.7 %collective-permute-done.1 = bf16[1280,768]{1,0:T(8,128)(2,1)} collective-permute-done((bf16[1280,768]{1,0:T(8,128)(2,1)}, bf16[1280,768]{1,0:T(8,128)(2,1)}, u32[]{:S(2)}, u32[]{:S(2)}) %collective-permute-start.1) | collective-permute-done | bytes 1966112 | tf_op jit(solution)/shard_map/ppermute | solution.py:21
  250.1 7.9 multiply_convert_fusion.1
  259.9 4.8 convolution_convert_fusion.1
  264.8 44.2 %reduce-scatter.7.cloned.1.call-done = bf16[640,768]{1,0:T(8,128)(2,1)} async-done(((bf16[2560,768]{1,0:T(8,128)(2,1)}), bf16[640,768]{1,0:T(8,128)(2,1)}) %reduce-scatter.7.cloned.1.call-update) | async-done | bytes 983056 | tf_op jit(solution)/shard_map/reduce_scatter | solution.py:181
  320.9 33.1 %all-gather.6.cloned.1.call-done = bf16[2560,768]{1,0:T(8,128)(2,1)} async-done(((bf16[640,768]{1,0:T(8,128)(2,1)}), bf16[2560,768]{1,0:T(8,128)(2,1)}) %all-gather.6.cloned.1.call-update) | async-done | bytes 3932176 | tf_op jit(solution)/shard_map/all_gather | solution.py:196
  354.0 9.6 %convert_reduce_fusion = (f32[768]{0:T(1024)}, bf16[2560,768]{1,0:T(8,128)(2,1)S(1)}) fusion(f32[2560,768]{1,0:T(8,128)} %get-tuple-element.261, f32[768]{0:T(1024)S(1)} %copy-done.37, bf16[2560,768]{1,0:T(8,128)(2,1)} %all-gather.6.cloned.1.call-done, bf16[768,768]{1,0:T(8,128)(2,1)} %param.37), kind=kOutput, calls=%fused_computation.53 | convolution fusion | flops 3045457152 | bytes 16914432 | tf_op jit(solution)/shard_map/gd,fd->gf/dot_general | solution.py:198
  365.5 4.8 convolution_convert_fusion
  370.5 42.8 %reduce-scatter.9.cloned.1.call-done = bf16[640,768]{1,0:T(8,128)(2,1)} async-done(((bf16[2560,768]{1,0:T(8,128)(2,1)}), bf16[640,768]{1,0:T(8,128)(2,1)}) %reduce-scatter.9.cloned.1.call-update) | async-done | bytes 983056 | tf_op jit(solution)/shard_map/reduce_scatter | solution.py:203
  419.8 8.2 fusion.41
  427.9 4.8 fusion.68
  432.7 20.2 %all-gather.8.cloned.1.call-done = bf16[2560,768]{1,0:T(8,128)(2,1)} async-done(((bf16[640,768]{1,0:T(8,128)(2,1)}), bf16[2560,768]{1,0:T(8,128)(2,1)}) %all-gather.8.cloned.1.call-update) | async-done | bytes 3932176 | tf_op jit(solution)/shard_map/all_gather | solution.py:216
  458.6 102.6 %while.23 = (s32[]{:T(128)}, bf16[5,512,576]{1,2,0:T(8,128)(2,1)}, bf16[5,512,192]{1,2,0:T(8,128)(2,1)}, s32[5,512]{1,0:T(8,128)S(1)}, s32[5]{0:T(128)}, /*index...) while((s32[]{:T(128)}, bf16[5,512,576]{1,2,0:T(8,128)(2,1)}, ...), condition=%wide.region_17.18_spmd, body=%wide.region_15.17_spmd.sunk | while | flops 517444096 | bytes 28075180 | solution.py:223
  468.1 4.7 fusion.144
  488.7 4.7 fusion.144
  493.3 4.4 fusion.143
  509.2 4.7 fusion.144
  529.7 4.7 fusion.144
  534.3 4.4 fusion.143
  550.2 4.7 fusion.144
  554.9 4.4 fusion.143
  561.2 4.8 copy.98
  570.1 6.0 convolution_bitcast_fusion.1
  578.0 5.8 convolution_convert_fusion.2
  586.4 11.0 %all-reduce = bf16[4608]{0:T(1024)(128)(2,1)S(1)} all-reduce(bf16[4608]{0:T(1024)(128)(2,1)S(1)} %convert_element_type.135), channel_id=6, replica_groups=mesh['dp'=8,'tensor'=4] {'tensor'}, use_global_device_ids=true, to_apply=%region_30.31.clone | all-reduce | flops 4608 | bytes 18432
  598.0 40.0 %all-reduce.1 = (f32[192]{0:T(256)}, f32[192]{0:T(256)}, f32[6,192]{1,0:T(8,128)S(1)}, f32[768]{0:T(1024)}) all-reduce(f32[192]{0:T(256)S(1)} %get-tuple-element.259, f32[192]{0:T(256)S(1)} %get-tuple-element.258, f32[6,192]{1,0:T(8,128)S(1)} %reshape.391, f32[768]{0:T(1024)S(1)} %copy-done.30), channel_id=1, replica_groups=mesh['dp'=8,'tensor'=4] {'dp'}, use_global_device_ids=true, to_apply=%region_21.22 | all-reduce | flops 2304 | bytes 18432 | tf_op jit(solution)/shard_map/psum | solution.py:271
  638.6 174.0 %all-reduce.5.cloned.1.call-done = (f32[768,576]{0,1:T(8,128)}, f32[192,768]{1,0:T(8,128)}, f32[768,768]{1,0:T(8,128)}, f32[768,768]{1,0:T(8,128)}) async-done(((f32[768,576]{0,1:T(8,128)}, f32[192,768]{1,0:T(8,128)}, f32[768,768]{1,0:T(8,128)}, f32[768,768]{1,0:T(8,128)}), (f32[768,576]{0,1:T(8,128)}, f32[192,768]{1,0:T(8,128)}, f32[768,768]{1,0:T(8,128)}, ...) | async-done | bytes 7077904 | tf_op jit(solution)/shard_map/psum | solution.py:271
  815.4 41.7 %reduce-scatter.11.cloned.1.call-done = bf16[640,768]{1,0:T(8,128)(2,1)} async-done(((bf16[2560,768]{1,0:T(8,128)(2,1)}), bf16[640,768]{1,0:T(8,128)(2,1)}) %reduce-scatter.11.cloned.1.call-update) | async-done | bytes 983056 | tf_op jit(solution)/shard_map/reduce_scatter | solution.py:253
  (290 shorter events, 193.3 us)
Async XLA Ops:
  7.2 242.9 %copy-start = (bf16[768,768]{1,0:T(8,128)(2,1)S(1)}, bf16[768,768]{1,0:T(8,128)(2,1)}, u32[]{:S(2)}) copy-start(bf16[768,768]{1,0:T(8,128)(2,1)} %param.35) | copy-start | bytes 3538948
  7.2 38.1 %all-gather.4.cloned.1.call-start = ((), (), s32[]{:S(2)}) async-start(), calls=%async_computation.4 | async-start | bytes 4915200 | tf_op jit(solution)/shard_map/all_gather | solution.py:149
  7.9 167.4 %reduce-scatter.5.cloned.1.call-start = ((), (), s32[]{:S(2)}) async-start(), calls=%async_computation.5 | async-start | bytes 9830400 | tf_op jit(solution)/shard_map/reduce_scatter | solution.py:167
  11.7 38.3 %copy-start.19 = (bf16[768,576]{0,1:T(8,128)(2,1)}, bf16[768,576]{0,1:T(8,128)(2,1)S(1)}, u32[]{:S(2)}) copy-start(bf16[768,576]{0,1:T(8,128)(2,1)S(1)} %constant_dynamic-update-slice_fusion.1) | copy-start | bytes 2654212
  11.7 39.3 %copy-start.33 = (f32[192]{0:T(256)S(1)}, f32[192]{0:T(256)}, u32[]{:S(2)}) copy-start(f32[192]{0:T(256)} %param.27) | copy-start | bytes 2308
  11.7 39.3 %copy-start.34 = (f32[192]{0:T(256)S(1)}, f32[192]{0:T(256)}, u32[]{:S(2)}) copy-start(f32[192]{0:T(256)} %param.30) | copy-start | bytes 2308
  60.1 41.8 %copy-start.18 = (bf16[192,768]{1,0:T(8,128)(2,1)S(1)}, bf16[192,768]{1,0:T(8,128)(2,1)}, u32[]{:S(2)}) copy-start(bf16[192,768]{1,0:T(8,128)(2,1)} %param.31) | copy-start | bytes 884740
  101.9 4.2 copy-start.8
  106.1 69.2 %copy-start.29 = (f32[768]{0:T(1024)S(1)}, f32[768]{0:T(1024)}, u32[]{:S(2)}) copy-start(f32[768]{0:T(1024)} %param.32) | copy-start | bytes 9220
  106.2 71.6 %copy-start.21 = (f32[768]{0:T(1024)S(1)}, f32[768]{0:T(1024)}, u32[]{:S(2)}) copy-start(f32[768]{0:T(1024)} %param.33) | copy-start | bytes 9220
  106.2 71.6 %copy-start.31 = (f32[768]{0:T(1024)S(1)}, f32[768]{0:T(1024)}, u32[]{:S(2)}) copy-start(f32[768]{0:T(1024)} %param.34) | copy-start | bytes 9220
  106.2 202.9 %reduce-scatter.7.cloned.1.call-start = ((), (), s32[]{:S(2)}) async-start(), calls=%async_computation.6 | async-start | bytes 4915200 | tf_op jit(solution)/shard_map/reduce_scatter | solution.py:181
  179.6 12.4 %collective-permute-start = (bf16[640,768]{1,0:T(8,128)(2,1)}, bf16[640,768]{1,0:T(8,128)(2,1)S(1)}, u32[]{:S(2)}, u32[]{:S(2)}) collective-permute-start(bf16[640,768]{1,0:T(8,128)(2,1)} %get-tuple-element.234), channel_id=1, source_target_pairs={{0,3},{1,0},{2,1},{3,2},{4,7},{5,4},{6,5},{7,6},{8,11},{9,8},{10,9... | collective-permute-start | bytes 2949128 | tf_op jit(solution)/shard_map/ppermute | solution.py:21
  195.5 45.4 %collective-permute-start.1 = (bf16[1280,768]{1,0:T(8,128)(2,1)}, bf16[1280,768]{1,0:T(8,128)(2,1)}, u32[]{:S(2)}, u32[]{:S(2)}) collective-permute-start(bf16[1280,768]{1,0:T(8,128)(2,1)} %pad_maximum_fusion), channel_id=1, source_target_pairs={{0,2},{1,3},{2,0},{3,1},{4,6},{5,7},{6,4},{7,5},{8,10},{9,11},{10,... | collective-permute-start | bytes 5898248 | tf_op jit(solution)/shard_map/ppermute | solution.py:21
  199.2 46.9 %copy-start.6 = (bf16[640,768]{1,0:T(8,128)(2,1)S(1)}, bf16[640,768]{1,0:T(8,128)(2,1)}, u32[]{:S(2)}) copy-start(bf16[640,768]{1,0:T(8,128)(2,1)} %copy-done.5) | copy-start | bytes 2949124
  250.1 9.8 %copy-start.36 = (bf16[768,768]{1,0:T(8,128)(2,1)S(1)}, bf16[768,768]{1,0:T(8,128)(2,1)}, u32[]{:S(2)}) copy-start(bf16[768,768]{1,0:T(8,128)(2,1)} %param.37) | copy-start | bytes 3538948
  264.7 44.3 %copy-start.20 = (f32[768]{0:T(1024)S(1)}, f32[768]{0:T(1024)}, u32[]{:S(2)}) copy-start(f32[768]{0:T(1024)} %param.38) | copy-start | bytes 9220
  264.7 48.4 %copy-start.22 = (f32[768]{0:T(1024)S(1)}, f32[768]{0:T(1024)}, u32[]{:S(2)}) copy-start(f32[768]{0:T(1024)} %param.39) | copy-start | bytes 9220
  264.7 48.4 %copy-start.32 = (f32[768]{0:T(1024)S(1)}, f32[768]{0:T(1024)}, u32[]{:S(2)}) copy-start(f32[768]{0:T(1024)} %param.40) | copy-start | bytes 9220
  264.7 89.2 %all-gather.6.cloned.1.call-start = ((), (), s32[]{:S(2)}) async-start(), calls=%async_computation.7 | async-start | bytes 4915200 | tf_op jit(solution)/shard_map/all_gather | solution.py:196
  309.0 4.1 copy-start.12
  320.8 92.5 %reduce-scatter.9.cloned.1.call-start = ((), (), s32[]{:S(2)}) async-start(), calls=%async_computation.8 | async-start | bytes 4915200 | tf_op jit(solution)/shard_map/reduce_scatter | solution.py:203
  370.3 82.6 %all-gather.8.cloned.1.call-start = ((), (), s32[]{:S(2)}) async-start(), calls=%async_computation.9 | async-start | bytes 4915200 | tf_op jit(solution)/shard_map/all_gather | solution.py:216
  419.7 393.0 %all-reduce.5.cloned.1.call-start = ((), (), s32[]{:S(2)}) async-start(), calls=%async_computation.11 | async-start | bytes 14155776 | tf_op jit(solution)/shard_map/psum | solution.py:271
  419.7 8.2 copy-start.35
  419.7 8.2 copy-start.40
  561.2 4.8 copy-start.9
  576.1 281.0 %reduce-scatter.11.cloned.1.call-start = ((), (), s32[]{:S(2)}) async-start(), calls=%async_computation.10 | async-start | bytes 4915200 | tf_op jit(solution)/shard_map/reduce_scatter | solution.py:253
  583.9 13.7 %copy-start.4 = (bf16[5,512,576]{1,2,0:T(8,128)(2,1)S(1)}, bf16[5,512,576]{1,2,0:T(8,128)(2,1)}, u32[]{:S(2)}) copy-start(bf16[5,512,576]{1,2,0:T(8,128)(2,1)} %get-tuple-element.109) | copy-start | bytes 8847364
  583.9 14.2 %copy-start.30 = (f32[768]{0:T(1024)S(1)}, f32[768]{0:T(1024)}, u32[]{:S(2)}) copy-start(f32[768]{0:T(1024)} %get-tuple-element.262) | copy-start | bytes 9220
  598.0 259.1 %copy-start.7 = (f32[640,768]{1,0:T(8,128)S(1)}, f32[640,768]{1,0:T(8,128)}, u32[]{:S(2)}) copy-start(f32[640,768]{1,0:T(8,128)} %get-tuple-element.232) | copy-start | bytes 5898244
  812.6 47.0 %copy-start.17 = (f32[192,768]{1,0:T(8,128)S(1)}, f32[192,768]{1,0:T(8,128)}, u32[]{:S(2)}) copy-start(f32[192,768]{1,0:T(8,128)} %get-tuple-element.450) | copy-start | bytes 1769476
  (24 other events, 50.8 us)
Sparse Core Ops, SparseCore 0:
  9.6 35.6 all-gather.3
  106.3 68.9 reduce-scatter.4
  264.9 44.1 reduce-scatter.6
  320.9 32.9 all-gather.5
  370.4 42.8 reduce-scatter.8
  419.8 33.0 all-gather.7
  576.2 236.3 all-reduce.4
  815.2 41.8 reduce-scatter.10
